TPU v7x, 32 devices: a whole 2x2x4 slice. The times are simulated.
32 devices in a mesh: gx: 8 (over z, x), gy: 4 (over y, core).
Axes of the slice: x: 2, y: 2, z: 4, core: 2. Of those that a mesh axis runs over, the one named last changes fastest.
Arguments:
- field: float32 [32, 384, 512], P(None, 'gx', 'gy'), may hold values from -3 to 6
- conductivity: float32 [32, 384, 512], P(None, 'gx', 'gy'), may hold values from 1 to 8
Outputs:
- updated: float32 [32, 384, 512], P(None, 'gx', 'gy')
All inputs are finite; a program needn't handle non-finite values.
Results may differ from a plain program's by a relative error of at most 0.004.
Values sent between devices are 32-bit elements; how exact they have to be, the bound alone decides.
A program may use at most 512 MiB of HBM per device.

v0:
```python
import jax
import jax.numpy as jnp
from jax import lax
from jax.sharding import PartitionSpec as P

depth_step = 8.0
implicit_weight = 0.5


def padded_2(cells, sides, width):
    for axis, dim in sides:
        count = lax.axis_size(axis)
        ends = count - 1
        head = lax.slice_in_dim(cells, 0, width, axis=dim)
        tail = lax.slice_in_dim(cells, cells.shape[dim] - width, cells.shape[dim], axis=dim)
        cells = jnp.concatenate(
            [
                lax.ppermute(tail, axis, [(i, (i + 1) % count) for i in range(ends)]),
                cells,
                lax.ppermute(head, axis, [((i + 1) % count, i) for i in range(ends)]),
            ],
            axis=dim,
        )
    return cells


def shifted(values, stride, axis):
    length = values.shape[axis]
    offset = abs(stride)
    sizes = list(values.shape)
    sizes[axis] = offset
    filler = jnp.zeros(tuple(sizes), values.dtype)
    if stride > 0:
        kept = lax.slice_in_dim(values, 0, length - offset, axis=axis)
        return jnp.concatenate([filler, kept], axis=axis)
    kept = lax.slice_in_dim(values, offset, length, axis=axis)
    return jnp.concatenate([kept, filler], axis=axis)


def local_sweeps(below, above, values):
    length = below.shape[0]
    factors = []
    knowns = []
    factor = above[0]
    known = values[:, 0]
    factors.append(factor)
    knowns.append(known)
    for place in range(1, length):
        divisor = 1.0 - below[place] * factor
        factor = above[place] / divisor
        known = (values[:, place] - below[place][None] * known) / divisor
        factors.append(factor)
        knowns.append(known)
    solved = [None] * length
    current = knowns[length - 1]
    solved[length - 1] = current
    for place in range(length - 2, -1, -1):
        current = knowns[place] - factors[place][None] * current
        solved[place] = current
    return jnp.stack(solved, axis=1)


def matrix_product(left, right):
    return jnp.stack(
        [
            left[0] * right[0] + left[1] * right[2],
            left[0] * right[1] + left[1] * right[3],
            left[2] * right[0] + left[3] * right[2],
            left[2] * right[1] + left[3] * right[3],
        ]
    )


def matrix_vector(left, vector):
    return jnp.stack(
        [left[0] * vector[0] + left[1] * vector[1], left[2] * vector[0] + left[3] * vector[1]]
    )


def initial_pack(coeffs):
    nothing = jnp.zeros_like(coeffs[0])
    return jnp.stack(
        [
            nothing,
            -coeffs[0],
            nothing,
            -coeffs[1],
            -coeffs[2],
            nothing,
            -coeffs[3],
            nothing,
            coeffs[4],
            coeffs[5],
        ]
    )


def block_sweeps(packed, count, fetch):
    stride = 1
    while stride < count:
        before, after = fetch(packed, stride)
        left_own, right_own, known_own = (packed[0:4], packed[4:8], packed[8:10])
        left_before, right_before, known_before = (before[0:4], before[4:8], before[8:10])
        left_after, right_after, known_after = (after[0:4], after[4:8], after[8:10])
        mixed = matrix_product(left_own, right_before) + matrix_product(right_own, left_after)
        entry_aa = 1.0 - mixed[0]
        entry_ab = -mixed[1]
        entry_ba = -mixed[2]
        entry_bb = 1.0 - mixed[3]
        determinant = entry_aa * entry_bb - entry_ab * entry_ba
        inverse = jnp.stack([entry_bb, -entry_ab, -entry_ba, entry_aa]) / determinant
        new_left = -matrix_product(left_own, left_before)
        new_right = -matrix_product(right_own, right_after)
        new_known = (
            known_own
            - matrix_vector(left_own, known_before)
            - matrix_vector(right_own, known_after)
        )
        packed = jnp.concatenate(
            [
                matrix_product(inverse, new_left),
                matrix_product(inverse, new_right),
                matrix_vector(inverse, new_known),
            ],
            axis=0,
        )
        stride = stride * 2
    return packed[8:10]


def along_blocks(packed, stride):
    return (shifted(packed, stride, 1), shifted(packed, -stride, 1))


def pick_near(solved, position):
    padded = jnp.pad(solved, ((0, 0), (1, 1), (0, 0)))
    near = lax.dynamic_slice_in_dim(padded, position, 3, 1)
    return (near[1, 0], near[0, 2])


def interface_x(coeffs):
    gathered = lax.all_gather(coeffs[:, None], "gx", axis=1, tiled=True)
    solved = block_sweeps(initial_pack(gathered), gathered.shape[1], along_blocks)
    return pick_near(solved, lax.axis_index("gx"))


def interface_y(coeffs):
    gathered = lax.all_gather(coeffs[:, None], "gy", axis=1, tiled=True)
    solved = block_sweeps(initial_pack(gathered), gathered.shape[1], along_blocks)
    return pick_near(solved, lax.axis_index("gy"))


def normalized(minus, plus, right_side, coupling):
    diagonal = 1.0 + coupling * (minus + plus)
    return (-coupling * minus / diagonal, -coupling * plus / diagonal, right_side / diagonal)


def solve_lines(minus, plus, right_side, interface, coupling):
    below, above, scaled = normalized(minus, plus, right_side, coupling)
    length, batch = below.shape
    blank = jnp.zeros((length - 1, batch), jnp.float32)
    left_source = jnp.concatenate([-below[0:1], blank], axis=0)
    right_source = jnp.concatenate([blank, -above[length - 1 : length]], axis=0)
    inner_below = jnp.concatenate([jnp.zeros((1, batch), jnp.float32), below[1:]], axis=0)
    inner_above = jnp.concatenate([above[: length - 1], jnp.zeros((1, batch), jnp.float32)], axis=0)
    local = local_sweeps(inner_below, inner_above, jnp.stack([scaled, left_source, right_source]))
    inside, from_left, from_right = (local[0], local[1], local[2])
    coeffs = jnp.stack(
        [
            from_left[0],
            from_left[length - 1],
            from_right[0],
            from_right[length - 1],
            inside[0],
            inside[length - 1],
        ]
    )
    before_value, after_value = interface(coeffs)
    return inside + from_left * before_value[None] + from_right * after_value[None]


def on_device(field, conductivity):
    count_z, count_x, count_y = field.shape
    total_x = count_x * lax.axis_size("gx")
    total_y = count_y * lax.axis_size("gy")
    x_couple = float(total_x * total_x // 16)
    y_couple = float(total_y * total_y // 16)
    padded = padded_2(jnp.stack([field, conductivity]), (("gx", 2), ("gy", 3)), 1)
    wide_field = padded[0]
    wide_cond = padded[1]
    minus_x = 0.5 * (conductivity + wide_cond[:, :-2, 1:-1])
    plus_x = 0.5 * (conductivity + wide_cond[:, 2:, 1:-1])
    minus_y = 0.5 * (conductivity + wide_cond[:, 1:-1, :-2])
    plus_y = 0.5 * (conductivity + wide_cond[:, 1:-1, 2:])
    minus_z = 0.5 * (conductivity + shifted(conductivity, 1, 0))
    plus_z = 0.5 * (conductivity + shifted(conductivity, -1, 0))
    flux_x = plus_x * (wide_field[:, 2:, 1:-1] - field) - minus_x * (
        field - wide_field[:, :-2, 1:-1]
    )
    flux_y = plus_y * (wide_field[:, 1:-1, 2:] - field) - minus_y * (
        field - wide_field[:, 1:-1, :-2]
    )
    flux_z = plus_z * (shifted(field, -1, 0) - field) - minus_z * (field - shifted(field, 1, 0))
    explicit = 2.0 * x_couple * flux_x + 2.0 * y_couple * flux_y + depth_step * flux_z

    def x_lines(values):
        return jnp.transpose(values, (1, 0, 2)).reshape(count_x, count_z * count_y)

    first_section = solve_lines(
        x_lines(minus_x), x_lines(plus_x), x_lines(explicit), interface_x, x_couple
    )
    first_section = jnp.transpose(first_section.reshape(count_x, count_z, count_y), (1, 0, 2))

    def y_lines(values):
        return jnp.transpose(values, (2, 0, 1)).reshape(count_y, count_z * count_x)

    second_section = solve_lines(
        y_lines(minus_y), y_lines(plus_y), y_lines(first_section), interface_y, y_couple
    )
    second_section = jnp.transpose(second_section.reshape(count_y, count_z, count_x), (1, 2, 0))
    below, above, scaled = normalized(
        minus_z.reshape(count_z, count_x * count_y),
        plus_z.reshape(count_z, count_x * count_y),
        second_section.reshape(count_z, count_x * count_y),
        implicit_weight * depth_step,
    )
    third_section = local_sweeps(below, above, scaled[None])[0].reshape(count_z, count_x, count_y)
    return field + third_section


def solution(mesh):
    return jax.shard_map(
        on_device,
        mesh=mesh,
        in_specs=(P(None, "gx", "gy"), P(None, "gx", "gy")),
        out_specs=P(None, "gx", "gy"),
        check_vma=False,
    )
```

profile of v0, /device:TPU:0, one launch (start us, length us, event | category | flops | bytes accessed | tf_op | source)
XLA Modules:
  0.0 1260.8 jit_solution(17227509657056265861)
XLA Ops:
  2.5 5.4 collective-permute-start
  12.9 4.6 copy.16973
  17.5 4.8 fusion.474
  38.8 4.1 collective-permute-start.2
  77.7 4.1 copy.17312
  81.8 4.0 copy.17310
  93.5 4.0 copy.17309
  106.4 14.8 %divide_bitcast_fusion.1 = (f32[48,32,128]{0,1,2:T(8,128)S(1)}, f32[48,32,128]{0,1,2:T(8,128)}, f32[48,32,128]{0,1,2:T(8,128)}, f32[32,48,128]{1,0,2:T(8,128)}, ...) fusion(f32[32,48,128]{1,0,2:T(8,128)} %copy-done.2, f32[32,48,128]{1,0,2:T(8,128)} %copy.17310, ...), kind=kLoop, calls=%fused_computation.154 | loop fusion | flops 8454144 | bytes 15679488 | tf_op jit(solution)/shard_map/div | solution.py:155
  136.8 8.6 fusion.471
  154.2 15.3 %slice_divide_fusion.4 = (f32[1,32,128]{0,1,2:T(8,128)}, f32[1,32,128]{0,1,2:T(8,128)}, f32[1,32,128]{0,1,2:T(8,128)}, f32[1,32,128]{0,1,2:T(8,128)}, f32[1,32,1...) fusion(f32[48,32,128]{0,1,2:T(8,128)S(1)} %copy-done, ...), kind=kLoop, calls=%fused_computation.1725 | loop fusion | flops 49152 | bytes 540672 | tf_op jit(solution)/shard_map/div | solution.py:50
  169.5 16.5 %fusion.469 = (f32[1,32,128]{0,1,2:T(8,128)}, f32[1,32,128]{0,1,2:T(8,128)}, f32[1,32,128]{0,1,2:T(8,128)}, f32[1,32,128]{0,1,2:T(8,128)}, f32[1,32,128]{0,1,2:T...) fusion(f32[48,32,128]{0,1,2:T(8,128)S(1)} %get-tuple-element.902), kind=kLoop, calls=%fused_computation.1770 | loop fusion | bytes 622592 | tf_op jit(solution)/shard_map/slice | solution.py:51
  186.0 16.5 %fusion.470 = (f32[1,32,128]{0,1,2:T(8,128)}, f32[1,32,128]{0,1,2:T(8,128)}, f32[1,32,128]{0,1,2:T(8,128)}, f32[1,32,128]{0,1,2:T(8,128)}, f32[1,32,128]{0,1,2:T...) fusion(f32[48,32,128]{0,1,2:T(8,128)S(1)} %get-tuple-element.902), kind=kLoop, calls=%fused_computation.1771 | loop fusion | bytes 622592 | tf_op jit(solution)/shard_map/slice | solution.py:51
  202.5 36.4 %fusion.472 = (f32[1,32,128]{0,1,2:T(8,128)}, f32[1,32,128]{0,1,2:T(8,128)}, f32[1,32,128]{0,1,2:T(8,128)}, f32[1,32,128]{0,1,2:T(8,128)}, f32[1,32,128]{0,1,2:T...) fusion(f32[48,32,128]{0,1,2:T(8,128)} %get-tuple-element.903), kind=kLoop, calls=%fused_computation.1773 | loop fusion | bytes 622592 | tf_op jit(solution)/shard_map/slice | solution.py:50
  239.0 16.3 %fusion.473 = (f32[1,32,128]{0,1,2:T(8,128)}, f32[1,32,128]{0,1,2:T(8,128)}, f32[1,32,128]{0,1,2:T(8,128)}, f32[1,32,128]{0,1,2:T(8,128)}, f32[1,32,128]{0,1,2:T...) fusion(f32[48,32,128]{0,1,2:T(8,128)S(1)} %copy-done.1), kind=kLoop, calls=%fused_computation.1774 | loop fusion | bytes 622592 | tf_op jit(solution)/shard_map/slice | solution.py:50
  503.6 4.7 subtract_divide_fusion.1
  508.7 5.0 fusion.277
  513.8 4.6 multiply_subtract_fusion.7
  519.2 34.9 %all-gather = f32[6,32768]{1,0:T(8,128)S(1)} all-gather(f32[6,4096]{1,0:T(8,128)S(1)} %stack.861), channel_id=2, replica_groups=mesh['gx'=8,'gy'=4] {'gx'}, dimensions={1}, use_global_device_ids=true | all-gather | bytes 884736 | tf_op jit(solution)/shard_map/all_gather | solution.py:142
  564.8 12.8 %stack.860 = f32[3,48,4096]{2,1,0:T(8,128)S(1)} concatenate(f32[3,1,4096]{2,1,0:T(1,128)} %copy-done.54, f32[3,1,4096]{2,1,0:T(1,128)} %get-tuple-element.725, f32[3,1,4096]{2,1,0:T(1,128)} %get-tuple-element.726, f32[3,1,4096]{2,1,0:T(1,128)} %get-tuple-element.727, f32[3,1,4096]{2,1,0:T(1,128)} %get-tuple-element.728, f32[3,1,4096]{2,1,0:T(1,128)} %get-tuple-element.729, ...), dimensions={1} | concatenate | bytes 4718592 | tf_op jit(solution)/shard_map/stack | solution.py:60
  587.5 6.8 bitcast_divide_fusion.3
  700.5 17.5 %slice_reduce_fusion.114 = (f32[3,1536]{1,0:T(4,128)S(1)}, f32[3,1536]{1,0:T(4,128)}, f32[3,1536]{1,0:T(4,128)S(1)}, f32[3,1536]{1,0:T(4,128)}, f32[3,1536]{1,0:...) fusion(f32[3,128,1536]{1,2,0:T(8,128)S(1)} %pad_maximum_fusion.2), kind=kLoop, calls=%fused_computation.127 | loop fusion | bytes 516096 | tf_op jit(solution)/shard_map/slice | solution.py:51
  718.0 23.7 %slice_reduce_fusion.96 = (f32[3,1536]{1,0:T(4,128)S(1)}, f32[3,1536]{1,0:T(4,128)S(1)}, f32[3,1536]{1,0:T(4,128)S(1)}, f32[3,1536]{1,0:T(4,128)S(1)}, f32[3,153...) fusion(f32[3,128,1536]{1,2,0:T(8,128)S(1)} %pad_maximum_fusion.2), kind=kLoop, calls=%fused_computation.109 | loop fusion | bytes 700416 | tf_op jit(solution)/shard_map/slice | solution.py:51
  741.8 24.4 %slice_reduce_fusion.76 = (f32[3,1536]{1,0:T(4,128)S(1)}, f32[3,1536]{1,0:T(4,128)S(1)}, f32[3,1536]{1,0:T(4,128)S(1)}, f32[3,1536]{1,0:T(4,128)S(1)}, f32[3,153...) fusion(f32[3,128,1536]{1,2,0:T(8,128)S(1)} %pad_maximum_fusion.2), kind=kLoop, calls=%fused_computation.89 | loop fusion | bytes 700416 | tf_op jit(solution)/shard_map/slice | solution.py:51
  766.2 24.0 %slice_reduce_fusion.38 = (f32[3,1536]{1,0:T(4,128)S(1)}, f32[3,1536]{1,0:T(4,128)S(1)}, f32[3,1536]{1,0:T(4,128)S(1)}, f32[3,1536]{1,0:T(4,128)S(1)}, f32[3,153...) fusion(f32[3,128,1536]{1,2,0:T(8,128)S(1)} %pad_maximum_fusion.2), kind=kLoop, calls=%fused_computation.51 | loop fusion | bytes 700416 | tf_op jit(solution)/shard_map/slice | solution.py:51
  790.2 24.4 %slice_reduce_fusion.20 = (f32[3,1536]{1,0:T(4,128)S(1)}, f32[3,1536]{1,0:T(4,128)S(1)}, f32[3,1536]{1,0:T(4,128)S(1)}, f32[3,1536]{1,0:T(4,128)S(1)}, f32[3,153...) fusion(f32[3,128,1536]{1,2,0:T(8,128)S(1)} %pad_maximum_fusion.2), kind=kLoop, calls=%fused_computation.33 | loop fusion | bytes 700416 | tf_op jit(solution)/shard_map/slice | solution.py:51
  814.6 24.4 %slice_reduce_fusion.58 = (f32[3,1536]{1,0:T(4,128)S(1)}, f32[3,1536]{1,0:T(4,128)}, f32[3,1536]{1,0:T(4,128)}, f32[3,1536]{1,0:T(4,128)S(1)}, f32[3,1536]{1,0:T...) fusion(f32[3,128,1536]{1,2,0:T(8,128)S(1)} %pad_maximum_fusion.2), kind=kLoop, calls=%fused_computation.71 | loop fusion | bytes 700416 | tf_op jit(solution)/shard_map/slice | solution.py:51
  839.2 24.9 %slice_reduce_fusion = (f32[3,1536]{1,0:T(4,128)}, f32[3,1536]{1,0:T(4,128)}, f32[3,1536]{1,0:T(4,128)}, f32[3,1536]{1,0:T(4,128)}, f32[3,1536]{1,0:T(4,128)}, /...) fusion(f32[3,128,1536]{1,2,0:T(8,128)S(1)} %pad_maximum_fusion.2), kind=kLoop, calls=%fused_computation.13 | loop fusion | bytes 700416 | tf_op jit(solution)/shard_map/slice | solution.py:51
  1060.2 4.7 multiply_subtract_fusion.253
  1068.6 3.9 multiply_subtract_fusion.163
  1076.3 5.6 all-gather.1
  1225.2 6.5 fusion.447
  1244.0 6.1 bitcast_divide_fusion
  (1794 shorter events, 840.6 us)
Async XLA Ops:
  2.5 25.8 %collective-permute-start = (f32[2,32,1,128]{3,1,2,0:T(8,128)}, f32[2,32,1,128]{3,1,2,0:T(8,128)}, u32[]{:S(2)}, u32[]{:S(2)}) collective-permute-start(f32[2,32,1,128]{3,1,2,0:T(8,128)} %get-tuple-element.1414), channel_id=1, source_target_pairs={{0,4},{4,8},{8,12},{12,16},{16,20},{20,24},{24,28},{1,5},{5,9},{9,... | collective-permute-start | bytes 98312 | tf_op jit(solution)/shard_map/ppermute | solution.py:18
  7.9 20.4 %collective-permute-start.1 = (f32[2,32,1,128]{3,1,2,0:T(8,128)}, f32[2,32,1,128]{3,1,2,0:T(8,128)}, u32[]{:S(2)}, u32[]{:S(2)}) collective-permute-start(f32[2,32,1,128]{3,1,2,0:T(8,128)} %get-tuple-element.1415), channel_id=1, source_target_pairs={{4,0},{8,4},{12,8},{16,12},{20,16},{24,20},{28,24},{5,1},{9,5},{13... | collective-permute-start | bytes 98312 | tf_op jit(solution)/shard_map/ppermute | solution.py:20
  37.6 31.4 %collective-permute-start.3 = (f32[2,32,50,1]{2,1,3,0:T(8,128)}, f32[2,32,50,1]{2,1,3,0:T(8,128)}, u32[]{:S(2)}, u32[]{:S(2)}) collective-permute-start(f32[2,32,50,1]{2,1,3,0:T(8,128)} %copy.16967), channel_id=1, source_target_pairs={{1,0},{2,1},{3,2},{5,4},{6,5},{7,6},{9,8},{10,9},{11,10},{13,12},{... | collective-permute-start | bytes 38408 | tf_op jit(solution)/shard_map/ppermute | solution.py:20
  38.8 26.8 %collective-permute-start.2 = (f32[2,32,50,1]{2,1,3,0:T(8,128)}, f32[2,32,50,1]{2,1,3,0:T(8,128)}, u32[]{:S(2)}, u32[]{:S(2)}) collective-permute-start(f32[2,32,50,1]{2,1,3,0:T(8,128)} %copy.16966), channel_id=1, source_target_pairs={{0,1},{1,2},{2,3},{4,5},{5,6},{6,7},{8,9},{9,10},{10,11},{12,13},{... | collective-permute-start | bytes 38408 | tf_op jit(solution)/shard_map/ppermute | solution.py:18
  275.7 225.1 %copy-start.204 = (f32[1,32,128]{2,1,0:T(8,128)}, f32[1,32,128]{2,1,0:T(8,128)S(1)}, u32[]{:S(2)}) copy-start(f32[1,32,128]{2,1,0:T(8,128)S(1)} %copy.17009) | copy-start | bytes 49156
  288.7 214.4 %copy-start.206 = (f32[1,32,128]{2,1,0:T(8,128)}, f32[1,32,128]{2,1,0:T(8,128)S(1)}, u32[]{:S(2)}) copy-start(f32[1,32,128]{2,1,0:T(8,128)S(1)} %copy.17008) | copy-start | bytes 49156
  293.4 209.7 %copy-start.207 = (f32[1,32,128]{2,1,0:T(8,128)}, f32[1,32,128]{2,1,0:T(8,128)S(1)}, u32[]{:S(2)}) copy-start(f32[1,32,128]{2,1,0:T(8,128)S(1)} %copy.17005) | copy-start | bytes 49156
  298.0 205.2 %copy-start.208 = (f32[1,32,128]{2,1,0:T(8,128)}, f32[1,32,128]{2,1,0:T(8,128)S(1)}, u32[]{:S(2)}) copy-start(f32[1,32,128]{2,1,0:T(8,128)S(1)} %copy.17002) | copy-start | bytes 49156
  304.1 199.1 %copy-start.209 = (f32[1,32,128]{2,1,0:T(8,128)}, f32[1,32,128]{2,1,0:T(8,128)S(1)}, u32[]{:S(2)}) copy-start(f32[1,32,128]{2,1,0:T(8,128)S(1)} %copy.16999) | copy-start | bytes 49156
  617.6 442.4 %copy-start.291 = (f32[1536]{0:T(1024)}, f32[1536]{0:T(1024)S(1)}, u32[]{:S(2)}) copy-start(f32[1536]{0:T(1024)S(1)} %mul.14162) | copy-start | bytes 18436
  619.1 440.9 %copy-start.292 = (f32[1536]{0:T(1024)}, f32[1536]{0:T(1024)S(1)}, u32[]{:S(2)}) copy-start(f32[1536]{0:T(1024)S(1)} %mul.14150) | copy-start | bytes 18436
  620.6 439.4 %copy-start.293 = (f32[1536]{0:T(1024)}, f32[1536]{0:T(1024)S(1)}, u32[]{:S(2)}) copy-start(f32[1536]{0:T(1024)S(1)} %mul.14138) | copy-start | bytes 18436
  622.1 437.9 %copy-start.294 = (f32[1536]{0:T(1024)}, f32[1536]{0:T(1024)S(1)}, u32[]{:S(2)}) copy-start(f32[1536]{0:T(1024)S(1)} %mul.14126) | copy-start | bytes 18436
  623.6 436.4 %copy-start.295 = (f32[1536]{0:T(1024)}, f32[1536]{0:T(1024)S(1)}, u32[]{:S(2)}) copy-start(f32[1536]{0:T(1024)S(1)} %mul.14114) | copy-start | bytes 18436
  625.1 434.9 %copy-start.296 = (f32[1536]{0:T(1024)}, f32[1536]{0:T(1024)S(1)}, u32[]{:S(2)}) copy-start(f32[1536]{0:T(1024)S(1)} %mul.14102) | copy-start | bytes 18436
  666.8 393.2 %copy-start.335 = (f32[1536]{0:T(1024)}, f32[1536]{0:T(1024)S(1)}, u32[]{:S(2)}) copy-start(f32[1536]{0:T(1024)S(1)} %mul.14090) | copy-start | bytes 18436
  668.3 391.7 %copy-start.337 = (f32[1536]{0:T(1024)}, f32[1536]{0:T(1024)S(1)}, u32[]{:S(2)}) copy-start(f32[1536]{0:T(1024)S(1)} %mul.14270) | copy-start | bytes 18436
  669.8 390.2 %copy-start.338 = (f32[1536]{0:T(1024)}, f32[1536]{0:T(1024)S(1)}, u32[]{:S(2)}) copy-start(f32[1536]{0:T(1024)S(1)} %mul.14258) | copy-start | bytes 18436
  671.3 388.7 %copy-start.340 = (f32[1536]{0:T(1024)}, f32[1536]{0:T(1024)S(1)}, u32[]{:S(2)}) copy-start(f32[1536]{0:T(1024)S(1)} %mul.14246) | copy-start | bytes 18436
  672.8 387.2 %copy-start.342 = (f32[1536]{0:T(1024)}, f32[1536]{0:T(1024)S(1)}, u32[]{:S(2)}) copy-start(f32[1536]{0:T(1024)S(1)} %mul.14234) | copy-start | bytes 18436
  674.4 385.7 %copy-start.344 = (f32[1536]{0:T(1024)}, f32[1536]{0:T(1024)S(1)}, u32[]{:S(2)}) copy-start(f32[1536]{0:T(1024)S(1)} %mul.14222) | copy-start | bytes 18436
  675.9 384.2 %copy-start.346 = (f32[1536]{0:T(1024)}, f32[1536]{0:T(1024)S(1)}, u32[]{:S(2)}) copy-start(f32[1536]{0:T(1024)S(1)} %mul.14210) | copy-start | bytes 18436
  677.4 382.7 %copy-start.348 = (f32[1536]{0:T(1024)}, f32[1536]{0:T(1024)S(1)}, u32[]{:S(2)}) copy-start(f32[1536]{0:T(1024)S(1)} %mul.14198) | copy-start | bytes 18436
  678.9 381.3 %copy-start.349 = (f32[1536]{0:T(1024)}, f32[1536]{0:T(1024)S(1)}, u32[]{:S(2)}) copy-start(f32[1536]{0:T(1024)S(1)} %mul.14186) | copy-start | bytes 18436
  680.4 379.8 %copy-start.351 = (f32[1536]{0:T(1024)}, f32[1536]{0:T(1024)S(1)}, u32[]{:S(2)}) copy-start(f32[1536]{0:T(1024)S(1)} %mul.14174) | copy-start | bytes 18436
  683.5 376.6 %copy-start.354 = (f32[1536]{0:T(1024)}, f32[1536]{0:T(1024)S(1)}, u32[]{:S(2)}) copy-start(f32[1536]{0:T(1024)S(1)} %mul.14306) | copy-start | bytes 18436
  685.0 375.2 %copy-start.355 = (f32[1536]{0:T(1024)}, f32[1536]{0:T(1024)S(1)}, u32[]{:S(2)}) copy-start(f32[1536]{0:T(1024)S(1)} %mul.14294) | copy-start | bytes 18436
  686.5 373.7 %copy-start.356 = (f32[1536]{0:T(1024)}, f32[1536]{0:T(1024)S(1)}, u32[]{:S(2)}) copy-start(f32[1536]{0:T(1024)S(1)} %mul.14282) | copy-start | bytes 18436
  864.8 200.8 %copy-start.301 = (f32[1536]{0:T(1024)}, f32[1536]{0:T(1024)S(1)}, u32[]{:S(2)}) copy-start(f32[1536]{0:T(1024)S(1)} %div.9730) | copy-start | bytes 18436
  865.6 200.1 %copy-start.304 = (f32[1536]{0:T(1024)}, f32[1536]{0:T(1024)S(1)}, u32[]{:S(2)}) copy-start(f32[1536]{0:T(1024)S(1)} %div.9722) | copy-start | bytes 18436
  867.7 192.4 %copy-start.307 = (f32[1536]{0:T(1024)}, f32[1536]{0:T(1024)S(1)}, u32[]{:S(2)}) copy-start(f32[1536]{0:T(1024)S(1)} %mul.14058) | copy-start | bytes 18436
  903.7 131.2 %copy-start.399 = (f32[1,32,48]{2,1,0:T(8,128)S(1)}, f32[1,32,48]{2,1,0:T(8,128)}, u32[]{:S(2)}) copy-start(f32[1,32,48]{2,1,0:T(8,128)} %get-tuple-element.1114) | copy-start | bytes 18436
  (409 other events, 12480.4 us)
where the time goes:
time: 1280 us; the launch traced here: 1260 us
  local copies, waits for them, and re-layouts  954 us (75%)
  other arithmetic  249 us (19%)
  blocking collectives  40.5 us (3%)
    slice x137, local copies, waits for them, and re-layouts, local_sweeps(): known = (values[:, place] - below[place][None] * known) / divisor  361 us
    slice x125, local copies, waits for them, and re-layouts, local_sweeps(): factor = above[place] / divisor  221 us
    squeeze x126, local copies, waits for them, and re-layouts, local_sweeps(): factor = above[place] / divisor  104 us
    unnamed x994, local copies, waits for them, and re-layouts  86.7 us
    unnamed x91, other arithmetic  81.2 us
    mul x127, local copies, waits for them, and re-layouts, local_sweeps(): known = (values[:, place] - below[place][None] * known) / divisor  63.1 us
    div x24, other arithmetic, local_sweeps(): factor = above[place] / divisor  48.2 us
    all_gather x1, blocking collectives, interface_x(): gathered = lax.all_gather(coeffs[:, None], 'gx', axis=1, tiled=True)  34.9 us
  transfers between devices with their start and end apart: 4, of which 0 were waited for; matrix products, arithmetic and copies ran while one was open for 4% of the time, Pallas kernels for 0%

commit v1 on v0

v1 whole, which is shorter than its diff:
```python
import functools

import jax
import jax.numpy as jnp
from jax import lax
from jax.experimental import pallas as pl
from jax.experimental.pallas import tpu as pltpu
from jax.sharding import PartitionSpec as P

MESH = pl.DeviceIdType.MESH
F32 = jnp.float32
depth_step = 8.0
implicit_weight = 0.5

LANES = 128
SUBS = 8
PAD = SUBS
X_CHUNKS = 4


def ceil8(rows):
    return (rows + 7) // 8 * 8


def eliminate_cell(state, g):
    a, h, ground_left = state
    q = 1.0 / (a + h + g)
    w = g * q
    p = h * q
    return (a * w, h * w, ground_left + a * p), (w, p, q)


def combine_coeffs(parts):
    count = len(parts)

    def ground(k):
        return parts[k][0] + parts[k + 1][2] if k + 1 < count else parts[k][0]

    a, h, left = ground(0), parts[0][1], parts[0][2]
    kept = []
    for k in range(count - 1):
        (passed, h, left), factors = eliminate_cell((a, h, left), parts[k + 1][1])
        a = ground(k + 1) + passed
        kept.append(factors)
    return (a, h, left), kept


def combine_sources(parts, kept):
    count = len(parts)

    def source(k):
        return parts[k][0] + parts[k + 1][1] if k + 1 < count else parts[k][0]

    r, left = source(0), parts[0][1]
    scaled = []
    for k in range(count - 1):
        w, p, q = kept[k]
        left = left + r * p
        scaled.append(r * q)
        r = source(k + 1) + r * w
    return (r, left), scaled


def expand(own, before, kept, scaled):
    values = [own]
    for k in range(len(kept) - 1, -1, -1):
        w, p, _ = kept[k]
        values.append(scaled[k] + p * before + w * values[-1])
    return values[::-1]


def global_coeffs(parts):
    count = len(parts)

    def ground(d):
        return parts[d][0] + parts[d + 1][2] if d + 1 < count else parts[d][0]

    e = ground(0) + parts[0][1]
    kept = []
    for d in range(count - 1):
        g = parts[d + 1][1]
        q = 1.0 / (e + g)
        w = g * q
        kept.append((w, q))
        e = ground(d + 1) + e * w
    kept.append((None, 1.0 / e))
    return kept


def global_solve(parts, kept):
    count = len(parts)

    def source(d):
        return parts[d][0] + parts[d + 1][1] if d + 1 < count else parts[d][0]

    r = source(0)
    scaled = []
    for d in range(count - 1):
        w, q = kept[d]
        scaled.append(r * q)
        r = source(d + 1) + r * w
    values = [r * kept[-1][1]]
    for d in range(count - 2, -1, -1):
        values.append(scaled[d] + kept[d][0] * values[-1])
    return values[::-1]


def kernel(
    sizes, f_ref, c_ref, out_ref,
    tf, tc, te, ts, tv, ex, fs,
    gyc, wy, py, qy, sy, scr, vo, vp, vnodes,
    gx_, wx, px, qx, sx, wz, qz,
    xs, xr, ys, yr, xc_s, xc_r, xr_s, xr_r, xv_s, xv_r, yc_s, yc_r, yr_s, yr_r,
    ssem, rsem,
):
    nz, nx, dx, dy, x_half, y_half, z_half = sizes
    rows = nz * nx
    blocks = rows // LANES
    span = LANES + 2 * PAD
    my = LANES // SUBS
    mx = nx // X_CHUNKS
    zc = nz // dx
    ix = lax.axis_index("gx")
    iy = lax.axis_index("gy")

    barrier = pltpu.get_barrier_semaphore()
    for k in range(1, dx):
        pl.semaphore_signal(
            barrier, inc=1, device_id={"gx": lax.rem(ix + k, dx)}, device_id_type=MESH
        )
    for k in range(1, dy):
        pl.semaphore_signal(
            barrier, inc=1, device_id={"gy": lax.rem(iy + k, dy)}, device_id_type=MESH
        )

    def remote(src, dst, at, target):
        return pltpu.make_async_remote_copy(
            src_ref=src, dst_ref=dst, send_sem=ssem.at[at], recv_sem=rsem.at[at],
            device_id=target, device_id_type=MESH,
        )

    for b in range(blocks):
        tf[pl.ds(b * span + PAD, LANES), :] = f_ref[pl.ds(b * LANES, LANES), :].T
        tc[pl.ds(b * span + PAD, LANES), :] = c_ref[pl.ds(b * LANES, LANES), :].T
    for side, place in ((0, nx - 1), (1, 0)):
        xs[side, 0] = f_ref[pl.ds(place, nz, stride=nx), :]
        xs[side, 1] = c_ref[pl.ds(place, nz, stride=nx), :]
    for side, place in ((0, LANES - 1), (1, 0)):
        ys[side, 0, :blocks] = tf[pl.ds(PAD + place, blocks, stride=span), :]
        ys[side, 1, :blocks] = tc[pl.ds(PAD + place, blocks, stride=span), :]

    pl.semaphore_wait(barrier, dx + dy - 2)

    x_up = remote(xs.at[0], xr.at[0], 0, {"gx": jnp.minimum(ix + 1, dx - 1)})
    x_down = remote(xs.at[1], xr.at[1], 1, {"gx": jnp.maximum(ix - 1, 0)})
    y_up = remote(ys.at[0], yr.at[0], 2, {"gy": jnp.minimum(iy + 1, dy - 1)})
    y_down = remote(ys.at[1], yr.at[1], 3, {"gy": jnp.maximum(iy - 1, 0)})
    for inside, copy in (
        (ix < dx - 1, x_up), (ix > 0, x_down), (iy < dy - 1, y_up), (iy > 0, y_down)
    ):
        pl.when(inside)(copy.start)

    def plane(ref, z):
        return ref[pl.ds(z * nx, nx), :]

    c_here, f_here = plane(c_ref, 0), plane(f_ref, 0)
    g = z_half * c_here
    excess = 1.0 + g
    flux = g * f_here
    for z in range(nz):
        if z + 1 < nz:
            c_next, f_next = plane(c_ref, z + 1), plane(f_ref, z + 1)
            g = z_half * (c_here + c_next)
            new_flux = g * (f_next - f_here)
        else:
            c_next, f_next = None, None
            g = z_half * c_here
            new_flux = -g * f_here
        q = 1.0 / (excess + g)
        w = g * q
        qz[pl.ds(z * nx, nx), :] = q
        wz[pl.ds(z * nx, nx), :] = w
        ex[pl.ds(z * nx, nx), :] = 2.0 * (new_flux - flux)
        excess = 1.0 + excess * w
        c_here, f_here, flux = c_next, f_next, new_flux

    def x_halo(side, inside, copy):
        pl.when(inside)(copy.wait_recv)

        @pl.when(jnp.logical_not(inside))
        def _():
            xr[side] = jnp.zeros(xr.shape[1:], F32)

    x_halo(0, ix > 0, x_up)
    x_halo(1, ix < dx - 1, x_down)

    def load_x(ref, which, j):
        pieces = []
        for k in range(X_CHUNKS):
            place = k * mx + j
            if place < 0:
                pieces.append(xr[0, which])
            elif place >= nx:
                pieces.append(xr[1, which])
            else:
                pieces.append(ref[pl.ds(place, nz, stride=nx), :])
        return jnp.concatenate(pieces, axis=0)

    c_here = load_x(c_ref, 1, 0)
    g = x_half * (load_x(c_ref, 1, -1) + c_here)
    gx_[0] = g
    state = (jnp.ones_like(g), g, jnp.zeros_like(g))
    for j in range(mx):
        c_next = load_x(c_ref, 1, j + 1)
        g = x_half * (c_here + c_next)
        gx_[j + 1] = g
        if j < mx - 1:
            (passed, h, left), (w, p, q) = eliminate_cell(state, g)
            wx[j], px[j], qx[j] = w, p, q
            state = (1.0 + passed, h, left)
        c_here = c_next

    def x_parts(arrays):
        return [tuple(v[k * nz : (k + 1) * nz] for v in arrays) for k in range(X_CHUNKS)]

    (a, h, left), x_kept = combine_coeffs(x_parts(state))
    a = a + jnp.where(ix == dx - 1, 1.0, 0.0) * g[(X_CHUNKS - 1) * nz :]
    for d in range(dx):
        for at, v in enumerate((a, h, left)):
            xc_s[d, at * zc : (at + 1) * zc] = v[d * zc : (d + 1) * zc]

    sems = [4]

    def spread(axis, count, src, dst):
        me = lax.axis_index(axis)
        copies = []
        for k in range(1, count):
            peer = lax.rem(me + k, count)
            piece = src.at[peer] if axis == "gx" else src
            copies.append(remote(piece, dst.at[me], sems[0], {axis: peer}))
            copies[-1].start()
            sems[0] += 1
        dst[me] = src[me] if axis == "gx" else src[...]
        return copies

    xc_copies = spread("gx", dx, xc_s, xc_r)

    def y_halo(side, inside, copy, place):
        pl.when(inside)(copy.wait_recv)

        @pl.when(jnp.logical_not(inside))
        def _():
            yr[side] = jnp.zeros(yr.shape[1:], F32)

        tf[pl.ds(place, blocks, stride=span), :] = yr[side, 0, :blocks]
        tc[pl.ds(place, blocks, stride=span), :] = yr[side, 1, :blocks]

    y_halo(0, iy > 0, y_up, PAD - 1)
    y_halo(1, iy < dy - 1, y_down, PAD + LANES)

    def load_y(ref, j, height, offset):
        return jnp.concatenate(
            [ref[pl.ds(b * height + offset + j, SUBS, stride=my), :] for b in range(blocks)],
            axis=0,
        )

    def store_y(ref, j, values):
        for b in range(blocks):
            ref[pl.ds(b * LANES + j, SUBS, stride=my), :] = values[b * SUBS : (b + 1) * SUBS]

    c_here, f_here = load_y(tc, 0, span, PAD), load_y(tf, 0, span, PAD)
    g = y_half * (load_y(tc, -1, span, PAD) + c_here)
    gyc[0] = g
    flux = g * (f_here - load_y(tf, -1, span, PAD))
    for j in range(my):
        c_next, f_next = load_y(tc, j + 1, span, PAD), load_y(tf, j + 1, span, PAD)
        g = y_half * (c_here + c_next)
        gyc[j + 1] = g
        new_flux = g * (f_next - f_here)
        store_y(te, j, 2.0 * (new_flux - flux))
        c_here, f_here, flux = c_next, f_next, new_flux
    for b in range(blocks):
        ex[pl.ds(b * LANES, LANES), :] += te[pl.ds(b * LANES, LANES), :].T

    f_here = load_x(f_ref, 0, 0)
    flux = gx_[0] * (f_here - load_x(f_ref, 0, -1))
    r = None
    for j in range(mx):
        f_next = load_x(f_ref, 0, j + 1)
        new_flux = gx_[j + 1] * (f_next - f_here)
        source = 2.0 * (new_flux - flux) + load_x(ex, None, j)
        if r is None:
            r, left = source, jnp.zeros_like(source)
        else:
            left = left + r * px[j - 1]
            sx[j - 1] = r * qx[j - 1]
            r = source + r * wx[j - 1]
        f_here, flux = f_next, new_flux
    (r, left), x_scaled = combine_sources(x_parts((r, left)), x_kept)
    for d in range(dx):
        for at, v in enumerate((r, left)):
            xr_s[d, at * zc : (at + 1) * zc] = v[d * zc : (d + 1) * zc]
    xr_copies = spread("gx", dx, xr_s, xr_r)

    g = gyc[0]
    state = (jnp.ones_like(g), g, jnp.zeros_like(g))
    for j in range(my - 1):
        (passed, h, left), (w, p, q) = eliminate_cell(state, gyc[j + 1])
        wy[j], py[j], qy[j] = w, p, q
        state = (1.0 + passed, h, left)

    def y_parts(arrays):
        for at, v in enumerate(arrays):
            scr[at] = v
        return [
            tuple(scr[at, pl.ds(s, blocks, stride=SUBS), :] for at in range(len(arrays)))
            for s in range(SUBS)
        ]

    parts = y_parts((*state, gyc[my]))
    (a, h, left), y_kept = combine_coeffs([part[:3] for part in parts])
    a = a + jnp.where(iy == dy - 1, 1.0, 0.0) * parts[-1][3]
    for at, v in enumerate((a, h, left)):
        yc_s[at, :blocks] = v
    yc_copies = spread("gy", dy, yc_s, yc_r)

    for copy in xc_copies:
        copy.wait_recv()
    x_global = global_coeffs(
        [tuple(xc_r[d, at * zc : (at + 1) * zc] for at in range(3)) for d in range(dx)]
    )
    for copy in xr_copies:
        copy.wait_recv()
    nodes = global_solve(
        [tuple(xr_r[d, at * zc : (at + 1) * zc] for at in range(2)) for d in range(dx)], x_global
    )
    for d in range(dx):
        xv_s[d, :zc] = nodes[d - 1] if d else jnp.zeros_like(nodes[0])
        xv_s[d, zc : 2 * zc] = nodes[d]
    xv_copies = spread("gx", dx, xv_s, xv_r)
    for copy in yc_copies:
        copy.wait_recv()
    y_global = global_coeffs(
        [tuple(yc_r[d, at, :blocks] for at in range(3)) for d in range(dy)]
    )
    for copy in xv_copies:
        copy.wait_recv()
    before = jnp.concatenate([xv_r[d, :zc] for d in range(dx)], axis=0)
    own = jnp.concatenate([xv_r[d, zc : 2 * zc] for d in range(dx)], axis=0)
    ends = expand(own, before, x_kept, x_scaled)
    v = jnp.concatenate(ends, axis=0)
    before = jnp.concatenate([before] + ends[:-1], axis=0)
    for j in range(mx - 1, -1, -1):
        if j < mx - 1:
            v = sx[j] + px[j] * before + wx[j] * v
        for k in range(X_CHUNKS):
            fs[pl.ds(k * mx + j, nz, stride=nx), :] = v[k * nz : (k + 1) * nz]

    for b in range(blocks):
        ts[pl.ds(b * LANES, LANES), :] = fs[pl.ds(b * LANES, LANES), :].T
    r = load_y(ts, 0, LANES, 0)
    left = jnp.zeros_like(r)
    for j in range(my - 1):
        left = left + r * py[j]
        sy[j] = r * qy[j]
        r = load_y(ts, j + 1, LANES, 0) + r * wy[j]
    (r, left), y_scaled = combine_sources(y_parts((r, left)), y_kept)
    yr_s[0, :blocks] = r
    yr_s[1, :blocks] = left
    yr_copies = spread("gy", dy, yr_s, yr_r)
    for copy in yr_copies:
        copy.wait_recv()
    nodes = global_solve(
        [tuple(yr_r[d, at, :blocks] for at in range(2)) for d in range(dy)], y_global
    )
    vnodes[0, :blocks] = jnp.zeros_like(nodes[0])
    for d in range(dy):
        vnodes[d + 1, :blocks] = nodes[d]
    before = vnodes[iy, :blocks]
    own = vnodes[iy + 1, :blocks]
    ends = expand(own, before, y_kept, y_scaled)
    for s in range(SUBS):
        vo[pl.ds(s, blocks, stride=SUBS), :] = ends[s]
        vp[pl.ds(s, blocks, stride=SUBS), :] = ends[s - 1] if s else before
    v = vo[...]
    before = vp[...]
    for j in range(my - 1, -1, -1):
        if j < my - 1:
            v = sy[j] + py[j] * before + wy[j] * v
        store_y(tv, j, v)
    for b in range(blocks):
        fs[pl.ds(b * LANES, LANES), :] = tv[pl.ds(b * LANES, LANES), :].T

    r = plane(fs, 0)
    for z in range(nz):
        fs[pl.ds(z * nx, nx), :] = r * plane(qz, z)
        if z + 1 < nz:
            r = plane(fs, z + 1) + r * plane(wz, z)
    v = None
    for z in range(nz - 1, -1, -1):
        v = plane(fs, z) if v is None else plane(fs, z) + plane(wz, z) * v
        out_ref[pl.ds(z * nx, nx), :] = plane(f_ref, z) + v

    for sent, copy in (
        (ix < dx - 1, x_up), (ix > 0, x_down), (iy < dy - 1, y_up), (iy > 0, y_down)
    ):
        pl.when(sent)(copy.wait_send)
    for copies in (xc_copies, xr_copies, xv_copies, yc_copies, yr_copies):
        for copy in copies:
            copy.wait_send()


def on_device(dx, dy, field, conductivity):
    nz, nx, ny = field.shape
    rows = nz * nx
    blocks = rows // LANES
    total_x = nx * dx
    total_y = ny * dy
    x_half = 0.5 * float(total_x * total_x // 16)
    y_half = 0.5 * float(total_y * total_y // 16)
    z_half = 0.5 * implicit_weight * depth_step
    zc = nz // dx
    span = LANES + 2 * PAD
    my = LANES // SUBS
    mx = nx // X_CHUNKS
    xrows = X_CHUNKS * nz
    yrows = blocks * SUBS
    b16 = ceil8(blocks)
    nsem = 4 + 3 * (dx - 1) + 2 * (dy - 1)

    def vmem(*shape):
        return pltpu.VMEM(shape, F32)

    grid = vmem(rows, LANES)
    out = pl.pallas_call(
        functools.partial(kernel, (nz, nx, dx, dy, x_half, y_half, z_half)),
        out_shape=jax.ShapeDtypeStruct((rows, LANES), F32),
        in_specs=[pl.BlockSpec(memory_space=pltpu.VMEM)] * 2,
        out_specs=pl.BlockSpec(memory_space=pltpu.VMEM),
        scratch_shapes=[
            vmem(blocks * span, LANES), vmem(blocks * span, LANES), grid, grid, grid, grid, grid,
            vmem(my + 1, yrows, LANES),
            vmem(my - 1, yrows, LANES), vmem(my - 1, yrows, LANES), vmem(my - 1, yrows, LANES),
            vmem(my - 1, yrows, LANES),
            vmem(4, yrows, LANES), vmem(yrows, LANES), vmem(yrows, LANES),
            vmem(dy + 1, b16, LANES),
            vmem(mx + 1, xrows, LANES),
            vmem(mx - 1, xrows, LANES), vmem(mx - 1, xrows, LANES), vmem(mx - 1, xrows, LANES),
            vmem(mx - 1, xrows, LANES),
            grid, grid,
            vmem(2, 2, nz, LANES), vmem(2, 2, nz, LANES),
            vmem(2, 2, b16, LANES), vmem(2, 2, b16, LANES),
            vmem(dx, ceil8(3 * zc), LANES), vmem(dx, ceil8(3 * zc), LANES),
            vmem(dx, ceil8(2 * zc), LANES), vmem(dx, ceil8(2 * zc), LANES),
            vmem(dx, ceil8(2 * zc), LANES), vmem(dx, ceil8(2 * zc), LANES),
            vmem(3, b16, LANES), vmem(dy, 3, b16, LANES),
            vmem(2, b16, LANES), vmem(dy, 2, b16, LANES),
            pltpu.SemaphoreType.DMA((nsem,)), pltpu.SemaphoreType.DMA((nsem,)),
        ],
        compiler_params=pltpu.CompilerParams(
            collective_id=0, has_side_effects=True, vmem_limit_bytes=48 << 20
        ),
    )(field.reshape(rows, ny), conductivity.reshape(rows, ny))
    return out.reshape(nz, nx, ny)


def solution(mesh):
    return jax.shard_map(
        functools.partial(on_device, mesh.shape["gx"], mesh.shape["gy"]),
        mesh=mesh,
        in_specs=(P(None, "gx", "gy"), P(None, "gx", "gy")),
        out_specs=P(None, "gx", "gy"),
        check_vma=False,
    )
```

time: 1280 us -> 27.8 us (0.02); the launches traced: 1260 us -> 27.6 us
  local copies, waits for them, and re-layouts: 954 us -> 3.15 us
  other arithmetic: 249 us -> 0 us
  blocking collectives: 40.5 us -> 0 us
  Pallas kernels: 0 us -> 24.5 us
    slice x296 -> x0, local copies, waits for them, and re-layouts: 610 us -> none  [the longest x137 361 us: local_sweeps(): known = (values[:, place] - below[place][None] * known) / divisor]
    squeeze x133 -> x0, local copies, waits for them, and re-layouts: 121 us -> none  [the longest x126 104 us: local_sweeps(): factor = above[place] / divisor]
    div x41 -> x0, other arithmetic: 90.2 us -> none  [the longest x24 48.2 us: local_sweeps(): factor = above[place] / divisor]
    unnamed x994 -> x5, local copies, waits for them, and re-layouts: 86.7 us -> 3.15 us
    unnamed x91 -> x0, other arithmetic: 81.2 us -> none
    mul x136 -> x0, local copies, waits for them, and re-layouts: 66.2 us -> none  [the longest x127 63.1 us: local_sweeps(): known = (values[:, place] - below[place][None] * known) / divisor]
    sub x31 -> x0, other arithmetic: 44.1 us -> none  [the longest x23 33.3 us: local_sweeps(): divisor = 1.0 - below[place] * factor]
    all_gather x2 -> x0, blocking collectives: 40.5 us -> none  [the longest x1 34.9 us: interface_x(): gathered = lax.all_gather(coeffs[:, None], 'gx', axis=1, tiled=True)]
  transfers between devices with their start and end apart: 4 -> 0, of which waited for: 0 -> 0; matrix products, arithmetic and copies ran while one was open for 4% -> 0% of each run, Pallas kernels for 0% -> 0%
where the time goes in v1:
time: 27.8 us; the launch traced here: 27.6 us
  Pallas kernels  24.5 us (88%)
  local copies, waits for them, and re-layouts  3.15 us (11%)
    pallas_call x1, Pallas kernels, on_device(): pl.pallas_call(functools.partial(kernel, (nz, nx, dx, dy, x_half, y_half,...  24.5 us
    unnamed x5, local copies, waits for them, and re-layouts  3.15 us

profile of v1, /device:TPU:0, one launch (start us, length us, event | category | flops | bytes accessed | tf_op | source)
XLA Modules:
  0.0 27.6 jit_solution(12108658217776415582)
XLA Ops:
  0.0 0.0 copy-start
  0.0 1.1 %copy-done = f32[32,48,128]{2,1,0:T(8,128)S(1)} copy-done((f32[32,48,128]{2,1,0:T(8,128)S(1)}, f32[32,48,128]{2,1,0:T(8,128)}, u32[]{:S(2)}) %copy-start) | copy-done | bytes 786456
  1.1 0.0 copy-start.1
  1.1 1.1 %copy-done.1 = f32[32,48,128]{2,1,0:T(8,128)S(1)} copy-done((f32[32,48,128]{2,1,0:T(8,128)S(1)}, f32[32,48,128]{2,1,0:T(8,128)}, u32[]{:S(2)}) %copy-start.1) | copy-done | bytes 786456
  2.3 24.5 %shard_map.28 = f32[1536,128]{1,0:T(8,128)S(1)} custom-call(f32[1536,128]{1,0:T(8,128)S(1)} %bitcast.4, f32[1536,128]{1,0:T(8,128)S(1)} %bitcast.5), custom_call_target="tpu_custom_call" | custom-call | tf_op jit(solution)/shard_map/pallas_call | solution.py:435
  26.7 0.9 %copy.4 = f32[32,48,128]{2,1,0:T(8,128)} copy(f32[32,48,128]{2,1,0:T(8,128)S(1)} %bitcast.3) | data formatting | bytes 1572864
Async XLA Ops:
  0.0 1.1 %copy-start = (f32[32,48,128]{2,1,0:T(8,128)S(1)}, f32[32,48,128]{2,1,0:T(8,128)}, u32[]{:S(2)}) copy-start(f32[32,48,128]{2,1,0:T(8,128)} %param.2) | copy-start | bytes 2359300
  1.1 1.1 %copy-start.1 = (f32[32,48,128]{2,1,0:T(8,128)S(1)}, f32[32,48,128]{2,1,0:T(8,128)}, u32[]{:S(2)}) copy-start(f32[32,48,128]{2,1,0:T(8,128)} %param.3) | copy-start | bytes 2359300

commit v2 on v1

--- a/solution.py
+++ b/solution.py
@@ -16,6 +16,8 @@
 SUBS = 8
 PAD = SUBS
 X_CHUNKS = 4
+LOADS = 4
+STORES = 4
 
 
 def ceil8(rows):
@@ -106,12 +108,13 @@
 
 
 def kernel(
-    sizes, f_ref, c_ref, out_ref,
+    sizes, f_hbm, c_hbm, out_hbm,
+    f_ref, c_ref, out_ref,
     tf, tc, te, ts, tv, ex, fs,
     gyc, wy, py, qy, sy, scr, vo, vp, vnodes,
     gx_, wx, px, qx, sx, wz, qz,
     xs, xr, ys, yr, xc_s, xc_r, xr_s, xr_r, xv_s, xv_r, yc_s, yc_r, yr_s, yr_r,
-    ssem, rsem,
+    ssem, rsem, lsem,
 ):
     nz, nx, dx, dy, x_half, y_half, z_half = sizes
     rows = nz * nx
@@ -133,6 +136,14 @@
             barrier, inc=1, device_id={"gy": lax.rem(iy + k, dy)}, device_id_type=MESH
         )
 
+    loads = []
+    piece = blocks // LOADS * LANES
+    for k in range(LOADS):
+        for at, (src, dst) in enumerate(((c_hbm, c_ref), (f_hbm, f_ref))):
+            part = pl.ds(k * piece, piece)
+            loads.append(pltpu.make_async_copy(src.at[part], dst.at[part], lsem.at[2 * k + at]))
+            loads[-1].start()
+
     def remote(src, dst, at, target):
         return pltpu.make_async_remote_copy(
             src_ref=src, dst_ref=dst, send_sem=ssem.at[at], recv_sem=rsem.at[at],
@@ -140,6 +151,10 @@
         )
 
     for b in range(blocks):
+        if b % (blocks // LOADS) == 0:
+            at = 2 * (b // (blocks // LOADS))
+            loads[at].wait()
+            loads[at + 1].wait()
         tf[pl.ds(b * span + PAD, LANES), :] = f_ref[pl.ds(b * LANES, LANES), :].T
         tc[pl.ds(b * span + PAD, LANES), :] = c_ref[pl.ds(b * LANES, LANES), :].T
     for side, place in ((0, nx - 1), (1, 0)):
@@ -148,17 +163,6 @@
     for side, place in ((0, LANES - 1), (1, 0)):
         ys[side, 0, :blocks] = tf[pl.ds(PAD + place, blocks, stride=span), :]
         ys[side, 1, :blocks] = tc[pl.ds(PAD + place, blocks, stride=span), :]
-
-    pl.semaphore_wait(barrier, dx + dy - 2)
-
-    x_up = remote(xs.at[0], xr.at[0], 0, {"gx": jnp.minimum(ix + 1, dx - 1)})
-    x_down = remote(xs.at[1], xr.at[1], 1, {"gx": jnp.maximum(ix - 1, 0)})
-    y_up = remote(ys.at[0], yr.at[0], 2, {"gy": jnp.minimum(iy + 1, dy - 1)})
-    y_down = remote(ys.at[1], yr.at[1], 3, {"gy": jnp.maximum(iy - 1, 0)})
-    for inside, copy in (
-        (ix < dx - 1, x_up), (ix > 0, x_down), (iy < dy - 1, y_up), (iy > 0, y_down)
-    ):
-        pl.when(inside)(copy.start)
 
     def plane(ref, z):
         return ref[pl.ds(z * nx, nx), :]
@@ -183,6 +187,17 @@
         ex[pl.ds(z * nx, nx), :] = 2.0 * (new_flux - flux)
         excess = 1.0 + excess * w
         c_here, f_here, flux = c_next, f_next, new_flux
+
+    pl.semaphore_wait(barrier, dx + dy - 2)
+
+    x_up = remote(xs.at[0], xr.at[0], 0, {"gx": jnp.minimum(ix + 1, dx - 1)})
+    x_down = remote(xs.at[1], xr.at[1], 1, {"gx": jnp.maximum(ix - 1, 0)})
+    y_up = remote(ys.at[0], yr.at[0], 2, {"gy": jnp.minimum(iy + 1, dy - 1)})
+    y_down = remote(ys.at[1], yr.at[1], 3, {"gy": jnp.maximum(iy - 1, 0)})
+    for inside, copy in (
+        (ix < dx - 1, x_up), (ix > 0, x_down), (iy < dy - 1, y_up), (iy > 0, y_down)
+    ):
+        pl.when(inside)(copy.start)
 
     def x_halo(side, inside, copy):
         pl.when(inside)(copy.wait_recv)
@@ -397,9 +412,15 @@
         if z + 1 < nz:
             r = plane(fs, z + 1) + r * plane(wz, z)
     v = None
+    stores = []
     for z in range(nz - 1, -1, -1):
         v = plane(fs, z) if v is None else plane(fs, z) + plane(wz, z) * v
         out_ref[pl.ds(z * nx, nx), :] = plane(f_ref, z) + v
+        if z % (nz // STORES) == 0:
+            part = pl.ds(z * nx, nz // STORES * nx)
+            at = 2 * LOADS + z // (nz // STORES)
+            stores.append(pltpu.make_async_copy(out_ref.at[part], out_hbm.at[part], lsem.at[at]))
+            stores[-1].start()
 
     for sent, copy in (
         (ix < dx - 1, x_up), (ix > 0, x_down), (iy < dy - 1, y_up), (iy > 0, y_down)
@@ -408,6 +429,8 @@
     for copies in (xc_copies, xr_copies, xv_copies, yc_copies, yr_copies):
         for copy in copies:
             copy.wait_send()
+    for copy in stores:
+        copy.wait()
 
 
 def on_device(dx, dy, field, conductivity):
@@ -435,9 +458,10 @@
     out = pl.pallas_call(
         functools.partial(kernel, (nz, nx, dx, dy, x_half, y_half, z_half)),
         out_shape=jax.ShapeDtypeStruct((rows, LANES), F32),
-        in_specs=[pl.BlockSpec(memory_space=pltpu.VMEM)] * 2,
-        out_specs=pl.BlockSpec(memory_space=pltpu.VMEM),
+        in_specs=[pl.BlockSpec(memory_space=pl.ANY)] * 2,
+        out_specs=pl.BlockSpec(memory_space=pl.ANY),
         scratch_shapes=[
+            grid, grid, grid,
             vmem(blocks * span, LANES), vmem(blocks * span, LANES), grid, grid, grid, grid, grid,
             vmem(my + 1, yrows, LANES),
             vmem(my - 1, yrows, LANES), vmem(my - 1, yrows, LANES), vmem(my - 1, yrows, LANES),
@@ -456,9 +480,10 @@
             vmem(3, b16, LANES), vmem(dy, 3, b16, LANES),
             vmem(2, b16, LANES), vmem(dy, 2, b16, LANES),
             pltpu.SemaphoreType.DMA((nsem,)), pltpu.SemaphoreType.DMA((nsem,)),
+            pltpu.SemaphoreType.DMA((2 * LOADS + STORES,)),
         ],
         compiler_params=pltpu.CompilerParams(
-            collective_id=0, has_side_effects=True, vmem_limit_bytes=48 << 20
+            collective_id=0, has_side_effects=True, vmem_limit_bytes=58 << 20
         ),
     )(field.reshape(rows, ny), conductivity.reshape(rows, ny))
     return out.reshape(nz, nx, ny)

time: 27.8 us -> 27.5 us (0.989)
  local copies, waits for them, and re-layouts: 3.15 us -> 2.06 us
  Pallas kernels: 24.5 us -> 25.3 us
    unnamed x5 -> x1, local copies, waits for them, and re-layouts: 3.15 us -> 2.06 us
    pallas_call x1, Pallas kernels: 24.5 us -> 25.3 us  [on_device(): pl.pallas_call(functools.partial(kernel, (nz, nx, dx, dy, x_half, y_half,...]
where the time goes in v2:
time: 27.5 us; the launch traced here: 27.4 us
  Pallas kernels  25.3 us (92%)
  local copies, waits for them, and re-layouts  2.06 us (7%)
    pallas_call x1, Pallas kernels, on_device(): pl.pallas_call(functools.partial(kernel, (nz, nx, dx, dy, x_half, y_half,...  25.3 us
    unnamed x1, local copies, waits for them, and re-layouts  2.06 us

profile of v2, /device:TPU:0, one launch (start us, length us, event | category | flops | bytes accessed | tf_op | source)
XLA Modules:
  0.0 27.4 jit_solution(638553155872288735)
XLA Ops:
  0.0 25.3 %shard_map.28 = f32[1536,128]{1,0:T(8,128)} custom-call(f32[1536,128]{1,0:T(8,128)} %bitcast.4, f32[1536,128]{1,0:T(8,128)} %bitcast.5), custom_call_target="tpu_custom_call" | custom-call | tf_op jit(solution)/shard_map/pallas_call | solution.py:458
  25.3 2.1 %copy.4 = f32[32,48,128]{2,1,0:T(8,128)} copy(f32[32,48,128]{2,1,0:T(8,128)} %bitcast.3) | data formatting | bytes 1572864

commit v3 on v2

--- a/solution.py
+++ b/solution.py
@@ -17,7 +17,6 @@
 PAD = SUBS
 X_CHUNKS = 4
 LOADS = 4
-STORES = 4
 
 
 def ceil8(rows):
@@ -108,8 +107,8 @@
 
 
 def kernel(
-    sizes, f_hbm, c_hbm, out_hbm,
-    f_ref, c_ref, out_ref,
+    sizes, f_hbm, c_hbm, out_ref,
+    f_ref, c_ref,
     tf, tc, te, ts, tv, ex, fs,
     gyc, wy, py, qy, sy, scr, vo, vp, vnodes,
     gx_, wx, px, qx, sx, wz, qz,
@@ -412,15 +411,9 @@
         if z + 1 < nz:
             r = plane(fs, z + 1) + r * plane(wz, z)
     v = None
-    stores = []
     for z in range(nz - 1, -1, -1):
         v = plane(fs, z) if v is None else plane(fs, z) + plane(wz, z) * v
         out_ref[pl.ds(z * nx, nx), :] = plane(f_ref, z) + v
-        if z % (nz // STORES) == 0:
-            part = pl.ds(z * nx, nz // STORES * nx)
-            at = 2 * LOADS + z // (nz // STORES)
-            stores.append(pltpu.make_async_copy(out_ref.at[part], out_hbm.at[part], lsem.at[at]))
-            stores[-1].start()
 
     for sent, copy in (
         (ix < dx - 1, x_up), (ix > 0, x_down), (iy < dy - 1, y_up), (iy > 0, y_down)
@@ -429,8 +422,6 @@
     for copies in (xc_copies, xr_copies, xv_copies, yc_copies, yr_copies):
         for copy in copies:
             copy.wait_send()
-    for copy in stores:
-        copy.wait()
 
 
 def on_device(dx, dy, field, conductivity):
@@ -459,9 +450,9 @@
         functools.partial(kernel, (nz, nx, dx, dy, x_half, y_half, z_half)),
         out_shape=jax.ShapeDtypeStruct((rows, LANES), F32),
         in_specs=[pl.BlockSpec(memory_space=pl.ANY)] * 2,
-        out_specs=pl.BlockSpec(memory_space=pl.ANY),
+        out_specs=pl.BlockSpec(memory_space=pltpu.VMEM),
         scratch_shapes=[
-            grid, grid, grid,
+            grid, grid,
             vmem(blocks * span, LANES), vmem(blocks * span, LANES), grid, grid, grid, grid, grid,
             vmem(my + 1, yrows, LANES),
             vmem(my - 1, yrows, LANES), vmem(my - 1, yrows, LANES), vmem(my - 1, yrows, LANES),
@@ -480,10 +471,10 @@
             vmem(3, b16, LANES), vmem(dy, 3, b16, LANES),
             vmem(2, b16, LANES), vmem(dy, 2, b16, LANES),
             pltpu.SemaphoreType.DMA((nsem,)), pltpu.SemaphoreType.DMA((nsem,)),
-            pltpu.SemaphoreType.DMA((2 * LOADS + STORES,)),
+            pltpu.SemaphoreType.DMA((2 * LOADS,)),
         ],
         compiler_params=pltpu.CompilerParams(
-            collective_id=0, has_side_effects=True, vmem_limit_bytes=58 << 20
+            collective_id=0, has_side_effects=True, vmem_limit_bytes=54016 << 10
         ),
     )(field.reshape(rows, ny), conductivity.reshape(rows, ny))
     return out.reshape(nz, nx, ny)

time: 27.5 us -> 25.5 us (0.927)
  local copies, waits for them, and re-layouts: 2.06 us -> 0.88 us
  Pallas kernels: 25.3 us -> 24.5 us
    unnamed x1, local copies, waits for them, and re-layouts: 2.06 us -> 0.88 us
    pallas_call x1, Pallas kernels: 25.3 us -> 24.5 us  [on_device(): pl.pallas_call(functools.partial(kernel, (nz, nx, dx, dy, x_half, y_half,...]
where the time goes in v3:
time: 25.5 us; the launch traced here: 25.4 us
  Pallas kernels  24.5 us (96%)
  local copies, waits for them, and re-layouts  0.88 us (3%)
    pallas_call x1, Pallas kernels, on_device(): pl.pallas_call(functools.partial(kernel, (nz, nx, dx, dy, x_half, y_half,...  24.5 us
    unnamed x1, local copies, waits for them, and re-layouts  0.88 us

profile of v3, /device:TPU:0, one launch (start us, length us, event | category | flops | bytes accessed | tf_op | source)
XLA Modules:
  0.0 25.4 jit_solution(14644992924859361467)
XLA Ops:
  0.0 24.5 %shard_map.28 = f32[1536,128]{1,0:T(8,128)S(1)} custom-call(f32[1536,128]{1,0:T(8,128)} %bitcast.4, f32[1536,128]{1,0:T(8,128)} %bitcast.5), custom_call_target="tpu_custom_call" | custom-call | tf_op jit(solution)/shard_map/pallas_call | solution.py:449
  24.5 0.9 %copy.4 = f32[32,48,128]{2,1,0:T(8,128)} copy(f32[32,48,128]{2,1,0:T(8,128)S(1)} %bitcast.3) | data formatting | bytes 1572864

commit v4 on v3

--- a/solution.py
+++ b/solution.py
@@ -162,6 +162,29 @@
     for side, place in ((0, LANES - 1), (1, 0)):
         ys[side, 0, :blocks] = tf[pl.ds(PAD + place, blocks, stride=span), :]
         ys[side, 1, :blocks] = tc[pl.ds(PAD + place, blocks, stride=span), :]
+
+    def load_y(ref, j, height, offset):
+        return jnp.concatenate(
+            [ref[pl.ds(b * height + offset + j, SUBS, stride=my), :] for b in range(blocks)],
+            axis=0,
+        )
+
+    def store_y(ref, j, values):
+        for b in range(blocks):
+            ref[pl.ds(b * LANES + j, SUBS, stride=my), :] = values[b * SUBS : (b + 1) * SUBS]
+
+    c_here, f_here = load_y(tc, 0, span, PAD), load_y(tf, 0, span, PAD)
+    y_first = y_last = None
+    for j in range(my - 1):
+        c_next, f_next = load_y(tc, j + 1, span, PAD), load_y(tf, j + 1, span, PAD)
+        g = y_half * (c_here + c_next)
+        gyc[j + 1] = g
+        new_flux = g * (f_next - f_here)
+        if j == 0:
+            y_first = new_flux
+        else:
+            store_y(te, j, 2.0 * (new_flux - y_last))
+        c_here, f_here, y_last = c_next, f_next, new_flux
 
     def plane(ref, z):
         return ref[pl.ds(z * nx, nx), :]
@@ -272,27 +295,14 @@
     y_halo(0, iy > 0, y_up, PAD - 1)
     y_halo(1, iy < dy - 1, y_down, PAD + LANES)
 
-    def load_y(ref, j, height, offset):
-        return jnp.concatenate(
-            [ref[pl.ds(b * height + offset + j, SUBS, stride=my), :] for b in range(blocks)],
-            axis=0,
-        )
-
-    def store_y(ref, j, values):
-        for b in range(blocks):
-            ref[pl.ds(b * LANES + j, SUBS, stride=my), :] = values[b * SUBS : (b + 1) * SUBS]
-
     c_here, f_here = load_y(tc, 0, span, PAD), load_y(tf, 0, span, PAD)
     g = y_half * (load_y(tc, -1, span, PAD) + c_here)
     gyc[0] = g
-    flux = g * (f_here - load_y(tf, -1, span, PAD))
-    for j in range(my):
-        c_next, f_next = load_y(tc, j + 1, span, PAD), load_y(tf, j + 1, span, PAD)
-        g = y_half * (c_here + c_next)
-        gyc[j + 1] = g
-        new_flux = g * (f_next - f_here)
-        store_y(te, j, 2.0 * (new_flux - flux))
-        c_here, f_here, flux = c_next, f_next, new_flux
+    store_y(te, 0, 2.0 * (y_first - g * (f_here - load_y(tf, -1, span, PAD))))
+    c_here, f_here = load_y(tc, my - 1, span, PAD), load_y(tf, my - 1, span, PAD)
+    g = y_half * (c_here + load_y(tc, my, span, PAD))
+    gyc[my] = g
+    store_y(te, my - 1, 2.0 * (g * (load_y(tf, my, span, PAD) - f_here) - y_last))
     for b in range(blocks):
         ex[pl.ds(b * LANES, LANES), :] += te[pl.ds(b * LANES, LANES), :].T
 

time: 25.5 us -> 24.8 us (0.973)
  Pallas kernels: 24.5 us -> 23.8 us
    pallas_call x1, Pallas kernels: 24.5 us -> 23.8 us  [on_device(): pl.pallas_call(functools.partial(kernel, (nz, nx, dx, dy, x_half, y_half,...]
where the time goes in v4:
time: 24.8 us; the launch traced here: 24.7 us
  Pallas kernels  23.8 us (96%)
  local copies, waits for them, and re-layouts  0.88 us (4%)
    pallas_call x1, Pallas kernels, on_device(): pl.pallas_call(functools.partial(kernel, (nz, nx, dx, dy, x_half, y_half,...  23.8 us
    unnamed x1, local copies, waits for them, and re-layouts  0.88 us

profile of v4, /device:TPU:0, one launch (start us, length us, event | category | flops | bytes accessed | tf_op | source)
XLA Modules:
  0.0 24.7 jit_solution(1504958346509733731)
XLA Ops:
  0.0 23.8 %shard_map.28 = f32[1536,128]{1,0:T(8,128)S(1)} custom-call(f32[1536,128]{1,0:T(8,128)} %bitcast.4, f32[1536,128]{1,0:T(8,128)} %bitcast.5), custom_call_target="tpu_custom_call" | custom-call | tf_op jit(solution)/shard_map/pallas_call | solution.py:459
  23.8 0.9 %copy.4 = f32[32,48,128]{2,1,0:T(8,128)} copy(f32[32,48,128]{2,1,0:T(8,128)S(1)} %bitcast.3) | data formatting | bytes 1572864
